TPU v7x, 512 devices: a whole 4x8x8 slice. The times are simulated.
512 devices in a mesh: replica: 32 (over x, z), tensor: 16 (over y, core).
Axes of the slice: x: 4, y: 8, z: 8, core: 2. Of those that a mesh axis runs over, the one named last changes fastest.
Arguments:
- tokens: bfloat16 [1536, 1536], P(('replica', 'tensor')), may hold values from -6 to 6
- attn_gain: float32 [1536], replicated, may hold values from 0.5 to 1.5
- qkv_weight: bfloat16 [1536, 2560], P(None, 'tensor'), may hold values from -0.15625 to 0.15625
- out_weight: bfloat16 [1536, 1536], P('tensor'), may hold values from -0.15625 to 0.15625
- moe_gain: float32 [1536], replicated, may hold values from 0.5 to 1.5
- router: bfloat16 [1536, 8], replicated, may hold values from -0.15625 to 0.15625
- expert_gate_up: bfloat16 [1536, 2, 4096], P(None, None, 'tensor'), may hold values from -0.15625 to 0.15625
- expert_down: bfloat16 [4096, 1536], P('tensor'), may hold values from -0.25 to 0.25
- kv_cache: bfloat16 [3072, 2, 128, 512], P(('replica', 'tensor')), may hold values from -240 to 240
- page_table: int32 [1024, 2], P('replica'), may hold values from 0 to 93, as said below
- home_len: int32 [1024], P('replica'), may hold values from 1 to 256
- guest_source: int32 [512], P(('replica', 'tensor')), may hold values from 0 to 31, as said below
- guest_pages: int32 [512, 2], P(('replica', 'tensor')), may hold values from 4 to 5, as said below
- guest_len: int32 [512], P(('replica', 'tensor')), may hold values from 1 to 256
- routes: int32 [1536, 6], P('replica'), may hold values from 0 to 7, all different within a row
Outputs:
- layer_out: bfloat16 [1536, 1536], P(('replica', 'tensor'))
Inputs may be any that keep to these rules, and one draw needn't show every extreme that they name: `page_table`: the home requests of one replica name different pages, together each of a device's first 4 pages exactly once. `guest_source`: never the guest's own replica; among the guests of one slot and one tensor index, each replica is named exactly once. `guest_pages`: each row names 2 different pages, none of them named by a home request, and guests of different slots name different pages.
All inputs are finite; a program needn't handle non-finite values.
Results may differ from a plain program's by a relative error of at most 0.022.
Values may be sent and summed in bfloat16 or wider, within the bound.
A program may use at most 64 MiB of HBM per device.

v0:
```python
import jax
import jax.numpy as jnp
from jax import lax
from jax.sharding import PartitionSpec as P

HEADS = 12
KVH = 4
HD = 128
MOE_FF = 512


def normed_rows(values, gain):
    widened = values.astype(jnp.float32)
    inverse = lax.rsqrt(jnp.mean(widened * widened, axis=-1, keepdims=True) + 1e-05)
    return (widened * inverse * gain).astype(jnp.bfloat16)


def page_terms(queries, page_ids, lengths, kv_cache, first_page):
    row_count, kv_heads, group_size, head_dim = queries.shape
    npages, _, page_len, _ = kv_cache.shape
    key_rows = kv_cache[:, 0].reshape(npages * page_len, kv_heads, head_dim)
    value_rows = kv_cache[:, 1].reshape(npages * page_len, kv_heads, head_dim)
    scores = jnp.einsum(
        "rkgd,jkd->rkgj", queries, key_rows, preferred_element_type=jnp.float32
    ) * head_dim ** (-0.5)
    holders = first_page + jnp.arange(npages, dtype=jnp.int32)
    offsets = jnp.arange(page_ids.shape[1], dtype=jnp.int32) * page_len
    inside = jnp.arange(page_len, dtype=jnp.int32)
    matches = page_ids[:, :, None] == holders[None, None, :]
    in_length = offsets[None, :, None] + inside[None, None, :] < lengths[:, None, None]
    usable = jnp.any(matches[:, :, :, None] & in_length[:, :, None, :], axis=1).reshape(
        row_count, npages * page_len
    )
    usable_mask = usable[:, None, None, :]
    scores = jnp.where(usable_mask, scores, -1e30)
    peaks = jnp.max(scores, axis=-1)
    weights = jnp.where(usable_mask, jnp.exp(scores - peaks[..., None]), 0.0)
    totals = jnp.sum(weights, axis=-1)
    summed = jnp.einsum(
        "rkgj,jkd->rkgd",
        weights.astype(jnp.bfloat16),
        value_rows,
        preferred_element_type=jnp.float32,
    )
    head_count = kv_heads * group_size
    return (
        summed.reshape(row_count, head_count * head_dim),
        peaks.reshape(row_count, head_count),
        totals.reshape(row_count, head_count),
    )


def combine_terms(summed, peaks, totals, queries, fresh_key, fresh_value):
    row_count, sources, head_count = peaks.shape
    kv_heads, group_size, head_dim = queries.shape[1:]
    own_score = jnp.einsum(
        "rkgd,rkd->rkg", queries, fresh_key, preferred_element_type=jnp.float32
    ).reshape(row_count, head_count) * head_dim ** (-0.5)
    highest = jnp.maximum(jnp.max(peaks, axis=1), own_score)
    factor = jnp.exp(peaks - highest[:, None, :])
    newest = jnp.exp(own_score - highest)
    spread = jnp.broadcast_to(
        fresh_value.astype(jnp.float32)[:, :, None, :], (row_count, kv_heads, group_size, head_dim)
    ).reshape(row_count, head_count, head_dim)
    numerator = (
        jnp.sum(
            summed.reshape(row_count, sources, head_count, head_dim) * factor[..., None], axis=1
        )
        + newest[..., None] * spread
    )
    denominator = jnp.sum(totals * factor, axis=1) + newest
    return (
        (numerator / denominator[..., None])
        .reshape(row_count, head_count * head_dim)
        .astype(jnp.bfloat16)
    )


def expert_terms(normed, chosen, router, gate_up, down_proj, first_unit):
    logits = jnp.dot(normed, router, preferred_element_type=jnp.float32)
    expert_count = router.shape[1]
    weights = jax.nn.softmax(jnp.take_along_axis(logits, chosen, axis=1), axis=1)
    labels = jnp.arange(expert_count, dtype=jnp.int32)
    expert_weight = jnp.sum(
        weights[:, :, None] * (chosen[:, :, None] == labels[None, None, :]), axis=1
    )
    unit_count = gate_up.shape[2]
    unit_owner = (first_unit + jnp.arange(unit_count, dtype=jnp.int32)) // MOE_FF
    per_unit = jnp.sum(
        expert_weight[:, :, None] * (unit_owner[None, None, :] == labels[None, :, None]), axis=1
    )
    both = jnp.einsum("td,dgu->tgu", normed, gate_up, preferred_element_type=jnp.float32)
    activated = (jax.nn.silu(both[:, 0]) * both[:, 1] * per_unit).astype(jnp.bfloat16)
    return jnp.dot(activated, down_proj, preferred_element_type=jnp.float32)


def shards(
    tokens,
    attn_gain,
    qkv_weight,
    out_weight,
    moe_gain,
    router,
    expert_gate_up,
    expert_down,
    kv_cache,
    page_table,
    home_len,
    guest_source,
    guest_pages,
    guest_len,
    routes,
):
    tensor_size = lax.axis_size("tensor")
    replica_count = lax.axis_size("replica")
    column = lax.axis_index("tensor")
    replica = lax.axis_index("replica")
    rows_dev = tokens.shape[0]
    home_dev = page_table.shape[0] // tensor_size
    guest_dev = guest_source.shape[0]
    kv_heads = KVH
    head_dim = HD
    group_size = HEADS // KVH
    qwidth = HEADS * HD
    kwidth = KVH * HD
    first_page = column * kv_cache.shape[0]
    all_rows = lax.all_gather(tokens, "tensor", axis=0, tiled=True)
    projected = jnp.dot(
        normed_rows(all_rows, attn_gain), qkv_weight, preferred_element_type=jnp.float32
    ).astype(jnp.bfloat16)
    joined = lax.all_gather(projected, "tensor", axis=1, tiled=True)
    layout = joined.reshape(tensor_size, rows_dev, joined.shape[1])
    home_q = layout[:, :home_dev, :qwidth].reshape(
        tensor_size * home_dev, kv_heads, group_size, head_dim
    )
    summed, peaks, totals = page_terms(home_q, page_table, home_len, kv_cache, first_page)
    own_rows = lax.dynamic_slice_in_dim(joined, column * rows_dev, rows_dev, 0)
    own_q = own_rows[:, :qwidth].reshape(rows_dev, kv_heads, group_size, head_dim)
    own_k = own_rows[:, qwidth : qwidth + kwidth].reshape(rows_dev, kv_heads, head_dim)
    own_v = own_rows[:, qwidth + kwidth :].reshape(rows_dev, kv_heads, head_dim)
    highest = lax.pmax(peaks, "tensor")
    factor = jnp.exp(peaks - highest)
    scaled = (summed.reshape(peaks.shape[0], peaks.shape[1], head_dim) * factor[..., None]).reshape(
        summed.shape
    )
    part_sum, part_total = (
        lax.psum_scatter(
            scaled.astype(jnp.bfloat16), "tensor", scatter_dimension=0, tiled=True
        ).astype(jnp.float32),
        lax.psum_scatter(
            (totals * factor).astype(jnp.bfloat16), "tensor", scatter_dimension=0, tiled=True
        ).astype(jnp.float32),
    )
    part_peak = lax.dynamic_slice_in_dim(highest, column * home_dev, home_dev, 0)
    home_out = combine_terms(
        part_sum[:, None],
        part_peak[:, None],
        part_total[:, None],
        own_q[:home_dev],
        own_k[:home_dev],
        own_v[:home_dev],
    )
    guest_q = own_rows[home_dev:, :qwidth]
    far_q, far_source, far_pages, far_len = (
        lax.all_gather(guest_q, "replica", axis=0, tiled=True),
        lax.all_gather(guest_source, "replica", axis=0, tiled=True),
        lax.all_gather(guest_pages, "replica", axis=0, tiled=True),
        lax.all_gather(guest_len, "replica", axis=0, tiled=True),
    )
    served = (far_source == replica).reshape(replica_count, guest_dev)
    picked = served[:, :, None]
    near_q = jnp.sum(
        jnp.where(picked, far_q.reshape(replica_count, guest_dev, qwidth).astype(jnp.float32), 0.0),
        axis=0,
    ).astype(jnp.bfloat16)
    near_pages = jnp.sum(
        jnp.where(picked, far_pages.reshape(replica_count, guest_dev, far_pages.shape[1]), 0),
        axis=0,
    ).astype(jnp.int32)
    near_len = jnp.sum(
        jnp.where(served, far_len.reshape(replica_count, guest_dev), 0), axis=0
    ).astype(jnp.int32)
    near_sum, near_peak, near_total = page_terms(
        near_q.reshape(guest_dev, kv_heads, group_size, head_dim),
        near_pages + first_page,
        near_len,
        kv_cache,
        first_page,
    )
    spread_sum = jnp.where(picked, near_sum[None], 0.0).reshape(
        replica_count * guest_dev, near_sum.shape[1]
    )
    spread_peak = jnp.where(picked, near_peak[None], 0.0).reshape(
        replica_count * guest_dev, near_peak.shape[1]
    )
    spread_total = jnp.where(picked, near_total[None], 0.0).reshape(
        replica_count * guest_dev, near_total.shape[1]
    )
    back_sum, back_peak, back_total = (
        lax.psum_scatter(
            spread_sum.astype(jnp.bfloat16), "replica", scatter_dimension=0, tiled=True
        ).astype(jnp.float32),
        lax.psum_scatter(
            spread_peak.astype(jnp.bfloat16), "replica", scatter_dimension=0, tiled=True
        ).astype(jnp.float32),
        lax.psum_scatter(
            spread_total.astype(jnp.bfloat16), "replica", scatter_dimension=0, tiled=True
        ).astype(jnp.float32),
    )
    guest_out = combine_terms(
        back_sum[:, None],
        back_peak[:, None],
        back_total[:, None],
        own_q[home_dev:],
        own_k[home_dev:],
        own_v[home_dev:],
    )
    attended = jnp.concatenate([home_out, guest_out], axis=0)
    columns = lax.all_to_all(attended, "tensor", split_axis=1, concat_axis=0, tiled=True)
    first_unit = column * expert_gate_up.shape[2]
    attn_sum = lax.psum_scatter(
        jnp.dot(columns, out_weight, preferred_element_type=jnp.float32).astype(jnp.bfloat16),
        "tensor",
        scatter_dimension=0,
        tiled=True,
    ).astype(jnp.float32)
    hidden = (tokens.astype(jnp.float32) + attn_sum).astype(jnp.bfloat16)
    expert_part = expert_terms(
        lax.all_gather(normed_rows(hidden, moe_gain), "tensor", axis=0, tiled=True),
        routes,
        router,
        expert_gate_up,
        expert_down,
        first_unit,
    )
    expert_out = lax.psum_scatter(
        expert_part.astype(jnp.bfloat16), "tensor", scatter_dimension=0, tiled=True
    ).astype(jnp.float32)
    return (hidden.astype(jnp.float32) + expert_out).astype(jnp.bfloat16)


def solution(mesh):
    placed = (
        P(("replica", "tensor"), None),
        P(),
        P(None, "tensor"),
        P("tensor", None),
        P(),
        P(),
        P(None, None, "tensor"),
        P("tensor", None),
        P(("replica", "tensor"), None, None, None),
        P("replica", None),
        P("replica"),
        P(("replica", "tensor")),
        P(("replica", "tensor"), None),
        P(("replica", "tensor")),
        P("replica", None),
    )
    return jax.shard_map(
        shards,
        mesh=mesh,
        in_specs=placed,
        out_specs=P(("replica", "tensor"), None),
        check_vma=False,
    )
```

profile of v0, /device:TPU:1, one launch (start us, length us, event | category | flops | bytes accessed | tf_op | source)
XLA Modules:
  0.0 639.7 jit_solution(10990740728805460668)
XLA Ops:
  6.6 21.8 %all-gather = bf16[16,3,1536]{2,1,0:T(4,128)(2,1)S(1)} all-gather(bf16[1,3,1536]{2,1,0:T(4,128)(2,1)} %bitcast.171), channel_id=1, replica_groups=mesh['replica'=32,'tensor'=16] {'tensor'}, dimensions={0}, use_global_device_ids=true | all-gather | bytes 156672 | tf_op jit(solution)/shard_map/all_gather | solution.py:127
  28.5 0.1 multiply_reduce_fusion.1
  28.7 1.0 fusion.7
  29.7 17.1 %all-gather.1 = bf16[16,160,48]{1,2,0:T(8,128)(2,1)S(1)} all-gather(bf16[1,160,48]{1,2,0:T(8,128)(2,1)S(1)} %fusion.7), channel_id=1, replica_groups=mesh['replica'=32,'tensor'=16] {'tensor'}, dimensions={0}, use_global_device_ids=true | all-gather | bytes 261120 | tf_op jit(solution)/shard_map/all_gather | solution.py:131
  46.9 0.5 reshape.584
  47.4 2.4 fusion.65
  49.9 1.7 reshape_squeeze.8
  51.6 1.1 reshape_squeeze.9
  52.7 0.1 reshape.553
  52.9 0.7 reshape.554
  53.9 0.1 and_reduce_fusion
  54.1 0.6 copy-done.6
  54.7 1.4 fusion.68
  56.0 0.6 reshape.555
  56.7 1.1 fusion.8
  57.7 0.6 reshape.557
  58.4 1.4 copy.128
  59.7 0.8 copy.127
  60.5 42.5 %pmax.7 = f32[32,12]{1,0:T(8,128)} all-reduce(f32[32,12]{1,0:T(8,128)S(1)} %copy.127), channel_id=1, replica_groups=mesh['replica'=32,'tensor'=16] {'tensor'}, use_global_device_ids=true, to_apply=%region_3.4 | all-reduce | flops 384 | bytes 3072 | tf_op jit(solution)/shard_map/pmax | solution.py:141
  103.0 1.6 convolution_bitcast_fusion
  104.6 0.1 copy.125
  104.9 0.7 multiply_convert_fusion.2
  105.8 0.7 fusion.18
  106.6 0.9 dynamic-slice_bitcast_fusion
  107.6 39.7 %all-gather.3 = bf16[32,1,1536]{2,1,0:T(2,128)(2,1)S(1)} all-gather(bf16[1,1,1536]{2,1,0:T(2,128)(2,1)S(1)} %get-tuple-element.22), channel_id=1, replica_groups=mesh['replica'=32,'tensor'=16] {'replica'}, dimensions={0}, use_global_device_ids=true | all-gather | bytes 101376 | tf_op jit(solution)/shard_map/all_gather | solution.py:165
  147.2 0.2 convert_element_type.167
  148.8 0.7 fusion.66
  149.4 0.7 dynamic-update-slice
  150.2 0.7 dynamic-update-slice.1
  150.9 15.5 %all-reduce.9 = (s32[32]{0:T(128)S(1)}, s32[32]{0:T(128)S(1)}) all-reduce(s32[32]{0:T(128)S(1)} %dynamic-update-slice, s32[32]{0:T(128)S(1)} %dynamic-update-slice.1), channel_id=1, replica_groups=mesh['replica'=32,'tensor'=16] {'replica'}, use_global_device_ids=true, to_apply=%add | all-reduce | flops 64 | bytes 512
  166.4 0.7 select_reduce_fusion.1
  167.3 0.7 broadcast_compare_fusion.2
  168.0 28.1 %all-gather.2 = s32[32,1,2]{2,1,0:T(1,128)S(1)} all-gather(s32[1,1,2]{2,1,0:T(1,128)S(1)} %bitcast.178), channel_id=1, replica_groups=mesh['replica'=32,'tensor'=16] {'replica'}, dimensions={0}, use_global_device_ids=true | all-gather | bytes 264 | tf_op jit(solution)/shard_map/all_gather | solution.py:167
  196.4 0.4 fusion.67
  196.9 0.3 convolution_bitcast_fusion.1
  197.2 0.7 select_convert_fusion
  198.0 0.2 fusion.26
  198.2 0.1 fusion.46
  198.7 111.1 %all-reduce.10 = (bf16[32,12]{1,0:T(8,128)(2,1)S(1)}, bf16[32,12]{1,0:T(8,128)(2,1)S(1)}) all-reduce(bf16[32,12]{1,0:T(8,128)(2,1)S(1)} %get-tuple-element.29, bf16[32,12]{1,0:T(8,128)(2,1)S(1)} %get-tuple-element.28), channel_id=6, replica_groups=mesh['replica'=32,'tensor'=16] {'replica'}, use_global_device_ids=true, to_apply=%region_15.16.clone | all-reduce | flops 768 | bytes 3072
  309.8 0.7 fusion.58
  310.5 0.7 fusion.50
  311.3 77.4 %all-reduce.3 = bf16[32,12]{0,1:T(8,128)(2,1)S(1)} all-reduce(bf16[32,12]{0,1:T(8,128)(2,1)S(1)} %copy.129), channel_id=3, replica_groups=mesh['replica'=32,'tensor'=16] {'tensor'}, use_global_device_ids=true, to_apply=%region_6.7.clone | all-reduce | flops 384 | bytes 1536
  388.7 1.2 dynamic-slice.3
  390.7 0.1 fusion.69
  390.9 0.7 multiply_add_fusion
  391.9 0.8 fusion.41
  392.8 1.4 convert_reduce_fusion
  394.3 0.6 pad_maximum_fusion
  394.9 5.5 all-to-all-start
  400.5 7.3 %all-to-all-done = bf16[3,16,96]{2,0,1:T(4,128)(2,1)S(1)} async-done(((bf16[3,16,96]{2,0,1:T(4,128)(2,1)}), bf16[3,16,96]{2,0,1:T(4,128)(2,1)S(1)}, u32[]{:S(2)}, u32[]{:S(2)}) %all-to-all-start) | async-done | bytes 9248 | tf_op jit(solution)/shard_map/all_to_all | solution.py:219
  407.8 0.8 convolution_convert_fusion.1
  409.5 94.5 %all-reduce.20.cloned.1.call-done = bf16[48,1536]{1,0:T(8,128)(2,1)} async-done(((bf16[48,1536]{1,0:T(8,128)(2,1)}), bf16[48,1536]{1,0:T(8,128)(2,1)}) %all-reduce.20.cloned.1.call-update) | async-done | bytes 147472
  504.0 0.9 fusion.30
  505.1 15.3 %all-gather.4 = bf16[16,3,1536]{2,1,0:T(4,128)(2,1)S(1)} all-gather(bf16[1,3,1536]{2,1,0:T(4,128)(2,1)S(1)} %fusion.39), channel_id=1, replica_groups=mesh['replica'=32,'tensor'=16] {'tensor'}, dimensions={0}, use_global_device_ids=true | all-gather | bytes 156672 | tf_op jit(solution)/shard_map/all_gather | solution.py:229
  520.4 0.1 reshape.590
  520.5 0.1 reshape.603
  520.7 0.1 fusion.70
  520.8 1.8 gather_fusion
  523.0 0.2 multiply_reduce_fusion
  523.2 0.4 fusion
  523.6 0.2 copy-done.3
  523.8 0.9 convolution_convert_fusion
  524.7 107.1 %all-reduce.22.cloned.1.call-done = bf16[48,1536]{1,0:T(8,128)(2,1)} async-done(((bf16[48,1536]{1,0:T(8,128)(2,1)}), bf16[48,1536]{1,0:T(8,128)(2,1)}) %all-reduce.22.cloned.1.call-update) | async-done | bytes 147472
  631.7 1.4 fusion.33
  (115 shorter events, 3.7 us)
Async XLA Ops:
  6.5 516.7 %copy-start = (bf16[1536,2,256]{2,1,0:T(2,128)(2,1)S(1)}, bf16[1536,2,256]{2,1,0:T(2,128)(2,1)}, u32[]{:S(2)}) copy-start(bf16[1536,2,256]{2,1,0:T(2,128)(2,1)} %param.21) | copy-start | bytes 4718596
  6.5 22.1 %copy-start.4 = (bf16[1536,160]{0,1:T(8,128)(2,1)S(1)}, bf16[1536,160]{0,1:T(8,128)(2,1)}, u32[]{:S(2)}) copy-start(bf16[1536,160]{0,1:T(8,128)(2,1)} %param.17) | copy-start | bytes 1474564
  6.5 385.3 %all-reduce.16.cloned.1.call-start = ((), (), s32[]{:S(2)}) async-start(), calls=%async_computation.1 | async-start | bytes 196608
  6.5 47.1 %copy-start.18 = (s32[2]{0:T(128)}, s32[2]{0:T(128)S(1)}, u32[]{:S(2)}) copy-start(s32[2]{0:T(128)S(1)} %iota_multiply_fusion) | copy-start | bytes 28
  47.4 5.3 copy-start.1
  51.6 2.2 copy-start.16
  51.6 2.1 copy-start.14
  51.6 2.2 copy-start.12
  54.0 0.6 copy-start.6
  56.0 2.3 copy-start.8
  104.8 44.0 %copy-start.13 = (u32[512]{0:T(512)S(1)}, u32[512]{0:T(512)}, u32[]{:S(2)}) copy-start(u32[512]{0:T(512)} %constant.102) | copy-start | bytes 6148
  104.8 62.5 %copy-start.19 = (s32[2]{0:T(128)S(1)}, s32[2]{0:T(128)}, u32[]{:S(2)}) copy-start(s32[2]{0:T(128)} %copy-done.18) | copy-start | bytes 28
  104.8 63.2 %copy-start.15 = (s32[1,2]{1,0:T(1,128)S(1)}, s32[1,2]{1,0:T(1,128)}, u32[]{:S(2)}) copy-start(s32[1,2]{1,0:T(1,128)} %param.27) | copy-start | bytes 28
  104.8 91.5 %copy-start.17 = (s32[6]{0:T(128)S(1)}, s32[6]{0:T(128)}, u32[]{:S(2)}) copy-start(s32[6]{0:T(128)} %copy-done.16) | copy-start | bytes 76
  105.8 91.0 %copy-start.2 = (bf16[768,4,128]{2,1,0:T(4,128)(2,1)S(1)}, bf16[768,4,128]{2,1,0:T(4,128)(2,1)}, u32[]{:S(2)}) copy-start(bf16[768,4,128]{2,1,0:T(4,128)(2,1)} %reshape_squeeze.9) | copy-start | bytes 2359300
  106.6 286.2 %all-reduce.18.cloned.1.call-start = ((), (), s32[]{:S(2)}) async-start(), calls=%async_computation.2 | async-start | bytes 196608
  196.4 211.4 %copy-start.5 = (bf16[96,1536]{1,0:T(8,128)(2,1)S(1)}, bf16[96,1536]{1,0:T(8,128)(2,1)}, u32[]{:S(2)}) copy-start(bf16[96,1536]{1,0:T(8,128)(2,1)} %param.18) | copy-start | bytes 884740
  196.8 211.9 %copy-start.7 = (s32[48,6]{0,1:T(8,128)S(1)}, s32[48,6]{0,1:T(8,128)}, u32[]{:S(2)}) copy-start(s32[48,6]{0,1:T(8,128)} %param.29) | copy-start | bytes 3460
  196.8 307.2 %copy-start.9 = (bf16[3,1536]{1,0:T(4,128)(2,1)S(1)}, bf16[3,1536]{1,0:T(4,128)(2,1)}, u32[]{:S(2)}) copy-start(bf16[3,1536]{1,0:T(4,128)(2,1)} %param.15) | copy-start | bytes 27652
  196.8 308.1 %copy-start.11 = (f32[1536]{0:T(1024)S(1)}, f32[1536]{0:T(1024)}, u32[]{:S(2)}) copy-start(f32[1536]{0:T(1024)} %param.19) | copy-start | bytes 18436
  198.2 322.5 %copy-start.10 = (bf16[1536,8]{0,1:T(8,128)(2,1)S(1)}, bf16[1536,8]{0,1:T(8,128)(2,1)}, u32[]{:S(2)}) copy-start(bf16[1536,8]{0,1:T(8,128)(2,1)} %param.20) | copy-start | bytes 73732
  394.9 12.9 %all-to-all-start = ((bf16[3,16,96]{2,0,1:T(4,128)(2,1)}), bf16[3,16,96]{2,0,1:T(4,128)(2,1)S(1)}, u32[]{:S(2)}, u32[]{:S(2)}) async-start(bf16[3,16,96]{2,0,1:T(4,128)(2,1)} %pad_maximum_fusion), calls=%async_computation | async-start | bytes 32768 | tf_op jit(solution)/shard_map/all_to_all | solution.py:219
  400.4 103.6 %all-reduce.20.cloned.1.call-start = ((), (), s32[]{:S(2)}) async-start(), calls=%async_computation.3 | async-start | bytes 294912
  408.7 223.1 %all-reduce.22.cloned.1.call-start = ((), (), s32[]{:S(2)}) async-start(), calls=%async_computation.4 | async-start | bytes 294912
  522.6 1.1 copy-start.3
Sparse Core Ops, SparseCore 0:
  106.7 112.8 all-reduce.15
  223.4 148.2 all-reduce.17
  408.8 95.2 all-reduce.19
  524.8 106.8 all-reduce.21
where the time goes:
time: 641 us; the launch traced here: 640 us
  blocking collectives  369 us (58%)
  waiting for transfers between devices  209 us (33%)
  local copies, waits for them, and re-layouts  19.8 us (3%)
  between operations  16 us (2%)
  other arithmetic  13.6 us (2%)
  matrix products  7.12 us (1%)
    unnamed x3, blocking collectives  204 us
    unnamed x8, waiting for transfers between devices  202 us
    pmax x1, blocking collectives, shards(): highest = lax.pmax(peaks, 'tensor')  42.5 us
    all_gather x1, blocking collectives, shards(): lax.all_gather(guest_q, 'replica', axis=0, tiled=True)  39.7 us
    all_gather x1, blocking collectives, shards(): lax.all_gather(guest_pages, 'replica', axis=0, tiled=True)  28.1 us
    all_gather x1, blocking collectives, shards(): all_rows = lax.all_gather(tokens, 'tensor', axis=0, tiled=True)  21.8 us
    all_gather x1, blocking collectives, shards(): joined = lax.all_gather(projected, 'tensor', axis=1, tiled=True)  17.1 us
    all_gather x1, blocking collectives, shards(): lax.all_gather(normed_rows(hidden, moe_gain), 'tensor', axis=0, tiled=True)  15.3 us
  transfers between devices with their start and end apart: 5, of which 3 were waited for; matrix products, arithmetic and copies ran while one was open for 2% of the time, Pallas kernels for 0%

commit v1 on v0

v1 whole, which is shorter than its diff:
```python
import functools

import jax
import jax.numpy as jnp
from jax import lax
from jax.experimental import pallas as pl
from jax.experimental.pallas import tpu as pltpu
from jax.sharding import PartitionSpec as P

MESH = pl.DeviceIdType.MESH
F32 = jnp.float32
BF16 = jnp.bfloat16
HEADS = 12
KVH = 4
HD = 128
PAGE = 128
TEN = 16
REP = 32
D = 1536
NEG = -1e30
SCALE = HD ** (-0.5)
FAR_FIRST = (8, 7, 9, 6, 10, 5, 11, 4, 12, 3, 13, 2, 14, 1, 15)


def replica_offsets():
    pairs = [(dx, dz) for dx in range(4) for dz in range(8) if (dx, dz) != (0, 0)]
    return sorted(pairs, key=lambda p: -(min(p[0], 4 - p[0]) + min(p[1], 8 - p[1])))


def iota(shape, dim):
    return lax.broadcasted_iota(jnp.int32, shape, dim)


def normed(rows, gain):
    inverse = lax.rsqrt(jnp.mean(rows * rows, axis=-1, keepdims=True) + 1e-05)
    return (rows * inverse * gain).astype(BF16)


def dot(a, b):
    return jnp.dot(a, b, preferred_element_type=F32)


def dot_t(a, b):
    return lax.dot_general(a, b, (((1,), (1,)), ((), ())), preferred_element_type=F32)


def per_head_rows(parts):
    kv_of = iota((16, HD), 0) // 3
    result = jnp.broadcast_to(parts[0], (16, HD))
    for k in range(1, KVH):
        result = jnp.where(kv_of == k, jnp.broadcast_to(parts[k], (16, HD)), result)
    return result


def block_queries(query):
    kv_of = iota((16, HD), 0) // 3
    return jnp.concatenate(
        [jnp.where(kv_of == k, query, 0.0) for k in range(KVH)], axis=1
    ).astype(BF16)


def own_lanes(wide):
    kv_of = iota((16, HD), 0) // 3
    result = wide[:, :HD]
    for k in range(1, KVH):
        result = jnp.where(kv_of == k, wide[:, k * HD : (k + 1) * HD], result)
    return result


def pack_terms(summed, peak, total):
    row, lane = iota((16, HD), 0), iota((16, HD), 1)
    live = row < HEADS
    spread = jnp.where(live & (lane == row), peak, 0.0) + jnp.where(
        live & (lane == row + 16), total, 0.0
    )
    stats = jnp.sum(spread, axis=0, keepdims=True)
    high = stats.astype(BF16).astype(F32)
    rest = stats - high
    middle = rest.astype(BF16).astype(F32)
    low = (rest - middle).astype(BF16).astype(F32)
    slab = jnp.where(live, summed, 0.0)
    for r, piece in ((12, high), (13, middle), (14, low)):
        slab = jnp.where(row == r, jnp.broadcast_to(piece, (16, HD)), slab)
    return slab.astype(BF16)


def unpack_terms(slab):
    row, lane = iota((16, HD), 0), iota((16, HD), 1)
    wide = slab.astype(F32)
    stats = jnp.broadcast_to(
        (wide[12:13] + wide[13:14]) + wide[14:15], (16, HD)
    )
    peak = jnp.sum(jnp.where(lane == row, stats, 0.0), axis=1, keepdims=True)
    total = jnp.sum(jnp.where(lane == row + 16, stats, 0.0), axis=1, keepdims=True)
    return wide, peak, total


def page_terms(query, keys, values, limits):
    blocks = block_queries(query)
    lane = iota((16, PAGE), 1)
    scores, usable = [], []
    for key, limit in zip(keys, limits):
        ok = lane < limit
        usable.append(ok)
        scores.append(jnp.where(ok, dot_t(blocks, key) * SCALE, NEG))
    peak = jnp.max(scores[0], axis=1, keepdims=True)
    for s in scores[1:]:
        peak = jnp.maximum(peak, jnp.max(s, axis=1, keepdims=True))
    weights = [jnp.where(ok, jnp.exp(s - peak), 0.0) for ok, s in zip(usable, scores)]
    total = sum(jnp.sum(w, axis=1, keepdims=True) for w in weights)
    wide = sum(dot(w.astype(BF16), v) for w, v in zip(weights, values))
    return own_lanes(wide), peak, total


def kernel(
    tok_ref, again_ref, mgain_ref, pt_ref, routes_ref,
    pt_s, hl_s, gs_s, gp_s, gl_s,
    wqkv_h, wo_h, router_h, wgu_h, wd_h, kv_h,
    out_ref,
    wqkv_v, wo_v, router_v, wgu_v, wd_v, kv_v,
    a_send, a_land, b_send, b_land, c_send, c_land, d_send, d_land,
    m_send, m_land, eh_send, eh_land, eg_send, eg_land,
    gh_send, gh_land, gg_send, gg_land, hh_send, hh_land, hg_send, hg_land,
    x_s, t_s, p_s, att_s, e_s, hid_s, y_s, mask_s,
    wsem, ssem, rsem,
):
    col = lax.axis_index("tensor")
    rep = lax.axis_index("replica")
    rx, rz = rep // 8, rep % 8
    ten_devs = [(k, (rep, lax.rem(col + k, TEN)), lax.rem(col + k, TEN)) for k in FAR_FIRST]
    rep_devs = [
        (lax.rem(rx + dx, 4) * 8 + lax.rem(rz + dz, 8), col) for dx, dz in replica_offsets()
    ]

    loads = [
        pltpu.make_async_copy(src, dst, wsem.at[i])
        for i, (src, dst) in enumerate(
            (
                (wqkv_h, wqkv_v), (kv_h, kv_v), (wgu_h, wgu_v),
                (wd_h, wd_v), (router_h, router_v),
            )
        )
    ]
    for load in loads:
        load.start()
    load_qkv, load_kv, load_gu, load_down, load_router = loads

    barrier = pltpu.get_barrier_semaphore()
    for dev in rep_devs:
        pl.semaphore_signal(barrier, inc=1, device_id=dev, device_id_type=MESH)
    for _, dev, _ in ten_devs:
        pl.semaphore_signal(barrier, inc=1, device_id=dev, device_id_type=MESH)

    def remote(src, dst, phase, dev):
        pltpu.make_async_remote_copy(
            src_ref=src, dst_ref=dst, send_sem=ssem.at[phase], recv_sem=rsem.at[phase],
            device_id=dev, device_id_type=MESH,
        ).start()

    def arrived(land, phase):
        pltpu.make_async_copy(land, land, rsem.at[phase]).wait()

    def gather(send, land, phase):
        for _, dev, _ in ten_devs:
            remote(send, land.at[col], phase, dev)
        pltpu.make_async_copy(send, land.at[col], rsem.at[phase]).start()

    def scatter(send, land, phase):
        for _, dev, other in ten_devs:
            remote(send.at[other], land.at[col], phase, dev)
        pltpu.make_async_copy(send.at[col], land.at[col], rsem.at[phase]).start()

    def gather_far(send, land, phase):
        for dev in rep_devs:
            remote(send, land.at[rep], phase, dev)
        pltpu.make_async_copy(send, land.at[rep], rsem.at[phase]).start()

    rows = tok_ref[...].astype(F32)
    a_send[:, :D] = rows[0:2].astype(BF16)
    a_send[:, D:] = jnp.concatenate(
        [rows[2:3, : D // 2], rows[2:3, D // 2 :]], axis=0
    ).astype(BF16)
    pl.semaphore_wait(barrier, TEN - 1 + REP - 1)
    gather(a_send, a_land, 0)

    lane, row = iota((32, 128), 1), iota((32, 128), 0)
    dest, place = lane >> 3, lane & 7
    target = jnp.where(place < 4, dest * 6 + place, -1)
    first, second = pt_ref[:, 0:1], pt_ref[:, 1:2]
    top = (
        (first == target)
        | (second == target)
        | ((place >= 4) & (place < 6) & (row == dest * 2 + place - 4))
    )
    glane, grow = iota((16, 128), 1), iota((16, 128), 0)
    bottom = ((glane & 7) == 6) & (grow == (glane >> 3))
    picks_t = jnp.concatenate(
        [
            jnp.where(top, 1.0, 0.0),
            jnp.where(bottom, 1.0, 0.0),
            jnp.zeros((80, 128), F32),
        ],
        axis=0,
    )
    picks = jnp.transpose(picks_t)[:, :48].astype(BF16)

    rlane = iota((48, 128), 1)
    routed = rlane < 0
    for k in range(6):
        routed = routed | (routes_ref[:, k : k + 1] == rlane)
    new, old = iota((48, 48), 0), iota((48, 48), 1)
    source_row = jnp.where(new < 32, (new >> 1) * 3 + (new & 1), (new - 32) * 3 + 2)
    order = jnp.where(old == source_row, 1.0, 0.0).astype(BF16)
    mask_s[...] = dot(order, jnp.where(routed, 1.0, 0.0).astype(BF16))

    base = col * 6

    def page_limits(j, limits):
        length = hl_s[j]
        one, two = pt_s[j, 0] - base, pt_s[j, 1] - base
        return tuple(
            limit + jnp.where(one == p, length, 0) + jnp.where(two == p, length - PAGE, 0)
            for p, limit in enumerate(limits)
        )

    limits = lax.fori_loop(0, 32, page_limits, (jnp.int32(0),) * 4)

    for _, dev, other in ten_devs:
        @pl.when(other < 12)
        def _():
            at = pl.multiple_of(other * 128, 128)
            remote(
                wo_h.at[:, pl.ds(at, 128)],
                wo_v.at[pl.ds(pl.multiple_of(col * 96, 96), 96), :],
                13, dev,
            )

    @pl.when(col < 12)
    def _():
        at = pl.multiple_of(col * 128, 128)
        pltpu.make_async_copy(
            wo_h.at[:, pl.ds(at, 128)],
            wo_v.at[pl.ds(pl.multiple_of(col * 96, 96), 96), :],
            rsem.at[13],
        ).start()

    arrived(a_land, 0)
    for c in range(TEN):
        slab = a_land[c].astype(F32)
        t_s[2 * c : 2 * c + 2, :] = slab[:, :D]
        t_s[32 + c : 33 + c, : D // 2] = slab[0:1, D:]
        t_s[32 + c : 33 + c, D // 2 :] = slab[1:2, D:]
    load_qkv.wait()
    projected = dot(normed(t_s[...], again_ref[...]), wqkv_v[...]).astype(BF16)
    chosen = dot(picks, projected)
    shift = lax.rem(col * 5, 4) * 32
    chosen = pltpu.roll(
        jnp.concatenate([chosen, jnp.zeros((128, 96), F32)], axis=1), shift, 1
    )
    for c in range(TEN):
        b_send[c] = chosen[8 * c : 8 * c + 8].astype(BF16)
    scatter(b_send, b_land, 1)

    arrived(b_land, 1)
    blocks = [None] * 20
    for c in range(TEN):
        slab = b_land[c].astype(F32)
        at = (5 * c) // 4
        for n, piece in ((at, slab[:, :128]), (at + 1, slab[:, 128:])):
            blocks[n] = piece if blocks[n] is None else blocks[n] + piece
    for n in range(20):
        p_s[8 * n : 8 * n + 8, :] = blocks[n]

    def heads_of(r):
        return p_s[pl.ds(r, 16, stride=8), :]

    def fresh_of(r, start):
        return per_head_rows([p_s[8 * (start + k) + r : 8 * (start + k) + r + 1, :] for k in range(KVH)])

    row16 = iota((16, HD), 0)
    slab = heads_of(6)
    for r, number in ((12, gs_s[0]), (13, gl_s[0]), (14, gp_s[0, 0]), (15, gp_s[0, 1])):
        slab = jnp.where(row16 == r, jnp.full((16, HD), number, jnp.int32).astype(F32), slab)
    c_send[...] = slab.astype(BF16)
    gather_far(c_send, c_land, 2)

    load_kv.wait()
    for p in range(4):
        summed, peak, total = page_terms(heads_of(p), [kv_v[p, 0]], [kv_v[p, 1]], [limits[p]])
        m_send[p] = pack_terms(summed, peak, total)
    gather(m_send, m_land, 4)

    arrived(c_land, 2)
    mine = jnp.full((16, HD), rep, jnp.int32).astype(F32)
    served = jnp.zeros((16, HD), F32)
    for r in range(REP):
        slab = c_land[r].astype(F32)
        served = jnp.where(jnp.broadcast_to(slab[12:13], (16, HD)) == mine, slab, served)
    length = served[13:14]
    page_a, page_b = served[14:15], served[15:16]
    far_limits = [
        jnp.broadcast_to(
            jnp.where(page_a == p, length, jnp.where(page_b == p, length - PAGE, 0.0)), (16, HD)
        ).astype(jnp.int32)
        for p in (4.0, 5.0)
    ]
    summed, peak, total = page_terms(
        served, [kv_v[4, 0], kv_v[5, 0]], [kv_v[4, 1], kv_v[5, 1]], far_limits
    )
    d_send[...] = pack_terms(summed, peak, total)
    gather_far(d_send, d_land, 3)

    def finish(r, terms):
        query = heads_of(r)
        own = jnp.sum(query * fresh_of(r, 12), axis=1, keepdims=True) * SCALE
        highest = own
        for _, peak, _ in terms:
            highest = jnp.maximum(highest, peak)
        newest = jnp.exp(own - highest)
        top_sum = newest * fresh_of(r, 16)
        bottom_sum = newest
        for summed, peak, total in terms:
            factor = jnp.exp(peak - highest)
            top_sum = top_sum + factor * summed
            bottom_sum = bottom_sum + factor * total
        return top_sum / bottom_sum

    arrived(m_land, 4)
    for s in range(2):
        terms = []
        for k in range(2):
            page = pt_s[2 * col + s, k]
            terms.append(unpack_terms(m_land[page // 6, page % 6]))
        att_s[16 * s : 16 * s + 16, :] = finish(4 + s, terms)
    eh_send[...] = jnp.concatenate(
        [att_s[pl.ds(h, 2, stride=16), :] for h in range(HEADS)], axis=1
    ).astype(BF16)
    gather(eh_send, eh_land, 5)

    arrived(d_land, 3)
    att_s[32:48, :] = finish(6, [unpack_terms(d_land[gs_s[0]])])
    eg_send[...] = jnp.concatenate(
        [att_s[pl.ds(32 + h, 2, stride=6), :] for h in range(HEADS // 2)], axis=1
    ).astype(BF16)
    gather(eg_send, eg_land, 6)

    mine_at = pl.multiple_of(jnp.where(col < 12, col, 0) * 128, 128)

    def to_columns(send, land, phase):
        for _, dev, _ in ten_devs:
            remote(send, land.at[col], phase, dev)
        pltpu.make_async_copy(send, land.at[col], rsem.at[phase]).start()

    def stage(land, start, guests):
        for c in range(TEN):
            slab = land[c].astype(F32)
            if guests:
                e_s[start + c : start + c + 1, : D // 2] = slab[0:1]
                e_s[start + c : start + c + 1, D // 2 :] = slab[1:2]
            else:
                e_s[start + 2 * c : start + 2 * c + 2, :] = slab

    arrived(eh_land, 5)

    @pl.when(col < 12)
    def _():
        arrived(wo_v, 13)
        stage(eh_land, 0, False)
        part = dot(e_s[0:32, :].astype(BF16), wo_v[...])
        gh_send[...] = (t_s[0:32, pl.ds(mine_at, 128)] + part).astype(BF16)
        to_columns(gh_send, gh_land, 7)

    arrived(eg_land, 6)

    @pl.when(col < 12)
    def _():
        stage(eg_land, 32, True)
        part = dot(e_s[32:48, :].astype(BF16), wo_v[...])
        gg_send[...] = (t_s[32:48, pl.ds(mine_at, 128)] + part).astype(BF16)
        to_columns(gg_send, gg_land, 8)

    def experts(land, start, count):
        hidden = jnp.concatenate([land[n] for n in range(12)], axis=1).astype(F32)
        hid_s[start : start + count, :] = hidden
        rows = normed(hidden, mgain_ref[...])
        logits = dot(rows, router_v[...])
        mask = mask_s[start : start + count, 0:8] > 0.5
        highest = jnp.max(jnp.where(mask, logits, NEG), axis=1, keepdims=True)
        powers = jnp.where(mask, jnp.exp(logits - highest), 0.0)
        here = jnp.where(iota((count, 8), 1) == col // 2, powers, 0.0)
        weight = jnp.sum(here, axis=1, keepdims=True) / jnp.sum(powers, axis=1, keepdims=True)
        both = dot(rows, wgu_v[...])
        gate, upper = both[:, :256], both[:, 256:]
        activated = (gate / (1.0 + jnp.exp(-gate)) * upper * weight).astype(BF16)
        y_s[start : start + count, :] = dot(activated, wd_v[...])

    arrived(gh_land, 7)
    load_router.wait()
    load_gu.wait()
    load_down.wait()
    experts(gh_land, 0, 32)
    for c in range(TEN):
        hh_send[c] = y_s[2 * c : 2 * c + 2, :].astype(BF16)
    scatter(hh_send, hh_land, 9)

    arrived(gg_land, 8)
    experts(gg_land, 32, 16)
    for c in range(TEN):
        hg_send[c] = jnp.concatenate(
            [y_s[32 + c : 33 + c, : D // 2], y_s[32 + c : 33 + c, D // 2 :]], axis=0
        ).astype(BF16)
    scatter(hg_send, hg_land, 10)

    def own_rows(start, at):
        tile = hid_s[pl.ds(pl.multiple_of(start + at // 8 * 8, 8), 8), :]
        return pltpu.roll(tile, lax.rem(8 - at % 8, 8), 0)

    arrived(hh_land, 9)
    total = hh_land[0].astype(F32)
    for c in range(1, TEN):
        total = total + hh_land[c].astype(F32)
    home = own_rows(0, 2 * col)[0:2] + total
    arrived(hg_land, 10)
    total = hg_land[0].astype(F32)
    for c in range(1, TEN):
        total = total + hg_land[c].astype(F32)
    guest = own_rows(32, col)[0:1] + jnp.concatenate([total[0:1], total[1:2]], axis=1)
    out_ref[...] = jnp.concatenate([home, guest], axis=0).astype(BF16)

    def left(land, count, phase):
        pltpu.make_async_copy(land.at[pl.ds(0, count)], land.at[pl.ds(0, count)], ssem.at[phase]).wait()

    for land, count, phase in (
        (a_land, 15, 0), (b_land, 15, 1), (c_land, 31, 2), (d_land, 31, 3), (m_land, 15, 4),
        (eh_land, 15, 5), (eg_land, 15, 6), (hh_land, 15, 9), (hg_land, 15, 10),
    ):
        left(land, count, phase)

    @pl.when(col < 12)
    def _():
        for src, dst, phase in ((gh_send, gh_land.at[0], 7), (gg_send, gg_land.at[0], 8)):
            for _ in range(15):
                pltpu.make_async_copy(src, dst, ssem.at[phase]).wait()
        pltpu.make_async_copy(wo_v.at[pl.ds(0, 96 * 11), :], wo_v.at[pl.ds(0, 96 * 11), :], ssem.at[13]).wait()

    @pl.when(col >= 12)
    def _():
        pltpu.make_async_copy(wo_v.at[pl.ds(0, 96 * 12), :], wo_v.at[pl.ds(0, 96 * 12), :], ssem.at[13]).wait()


def shards(
    tokens, attn_gain, qkv_weight, out_weight, moe_gain, router, expert_gate_up,
    expert_down, kv_cache, page_table, home_len, guest_source, guest_pages, guest_len, routes,
):
    vmem = pl.BlockSpec(memory_space=pltpu.VMEM)
    smem = pl.BlockSpec(memory_space=pltpu.SMEM)
    hbm = pl.BlockSpec(memory_space=pl.ANY)
    V = pltpu.VMEM
    return pl.pallas_call(
        kernel,
        out_shape=jax.ShapeDtypeStruct((3, D), BF16),
        in_specs=[vmem] * 5 + [smem] * 5 + [hbm] * 6,
        out_specs=vmem,
        scratch_shapes=[
            V((D, 160), BF16), V((D, 128), BF16), V((D, 8), BF16), V((D, 512), BF16),
            V((256, D), BF16), V((6, 2, 128, 512), BF16),
            V((2, 2304), BF16), V((TEN, 2, 2304), BF16),
            V((TEN, 8, 256), BF16), V((TEN, 8, 256), BF16),
            V((16, 128), BF16), V((REP, 16, 128), BF16),
            V((16, 128), BF16), V((REP, 16, 128), BF16),
            V((4, 16, 128), BF16), V((TEN, 4, 16, 128), BF16),
            V((2, D), BF16), V((TEN, 2, D), BF16),
            V((2, D // 2), BF16), V((TEN, 2, D // 2), BF16),
            V((32, 128), BF16), V((12, 32, 128), BF16),
            V((16, 128), BF16), V((12, 16, 128), BF16),
            V((TEN, 2, D), BF16), V((TEN, 2, D), BF16),
            V((TEN, 2, D // 2), BF16), V((TEN, 2, D // 2), BF16),
            V((8, 128), F32), V((48, D), F32), V((160, 128), F32), V((48, 128), F32),
            V((48, D), F32), V((48, D), F32), V((48, D), F32), V((48, 128), F32),
            pltpu.SemaphoreType.DMA((5,)),
            pltpu.SemaphoreType.DMA((14,)),
            pltpu.SemaphoreType.DMA((14,)),
        ],
        compiler_params=pltpu.CompilerParams(
            collective_id=0, has_side_effects=True, vmem_limit_bytes=48 << 20
        ),
    )(
        tokens, attn_gain.reshape(1, D), moe_gain.reshape(1, D), page_table, routes,
        page_table, home_len, guest_source, guest_pages, guest_len,
        qkv_weight, out_weight, router, expert_gate_up.reshape(D, 512), expert_down, kv_cache,
    )


def solution(mesh):
    placed = (
        P(("replica", "tensor"), None),
        P(),
        P(None, "tensor"),
        P("tensor", None),
        P(),
        P(),
        P(None, None, "tensor"),
        P("tensor", None),
        P(("replica", "tensor"), None, None, None),
        P("replica", None),
        P("replica"),
        P(("replica", "tensor")),
        P(("replica", "tensor"), None),
        P(("replica", "tensor")),
        P("replica", None),
    )
    return jax.shard_map(
        shards,
        mesh=mesh,
        in_specs=placed,
        out_specs=P(("replica", "tensor"), None),
        check_vma=False,
    )
```

time: 641 us -> 71.2 us (0.11)
  blocking collectives: 369 us -> 0 us
  waiting for transfers between devices: 209 us -> 0 us
  Pallas kernels: 0 us -> 61.9 us
  between operations: 16 us -> 1.5 us
  other arithmetic: 13.6 us -> 0 us
  local copies, waits for them, and re-layouts: 19.8 us -> 7.43 us
  matrix products: 7.12 us -> 0 us
    unnamed x3 -> x0, blocking collectives: 204 us -> none
    unnamed x8 -> x0, waiting for transfers between devices: 202 us -> none
    all_gather x5 -> x0, blocking collectives: 122 us -> none  [the longest x1 39.7 us: shards(): lax.all_gather(guest_q, 'replica', axis=0, tiled=True)]
    pallas_call x0 -> x1, Pallas kernels: none -> 61.9 us  [shards(): pl.pallas_call(kernel, out_shape=jax.ShapeDtypeStruct((3, D), BF16), in_s...]
    pmax x1 -> x0, blocking collectives: 42.5 us -> none  [shards(): highest = lax.pmax(peaks, 'tensor')]
    all_to_all x1 -> x0, waiting for transfers between devices: 7.27 us -> none  [shards(): lax.all_to_all(attended, 'tensor', split_axis=1, concat_axis=0, tiled=True)]
    dot_general x11 -> x0, matrix products: 7.12 us -> none  [the longest x2 1.87 us: page_terms(): jnp.einsum('rkgj,jkd->rkgd', weights.astype(jnp.bfloat16), value_rows, pr...]
  transfers between devices with their start and end apart: 5 -> 0, of which waited for: 3 -> 0; matrix products, arithmetic and copies ran while one was open for 2% -> 0% of each run, Pallas kernels for 0% -> 0%
where the time goes in v1:
time: 71.2 us; the launch traced here: 70.8 us
  Pallas kernels  61.9 us (87%)
  local copies, waits for them, and re-layouts  7.43 us (10%)
  between operations  1.5 us (2%)
    pallas_call x1, Pallas kernels, shards(): pl.pallas_call(kernel, out_shape=jax.ShapeDtypeStruct((3, D), BF16), in_s...  61.9 us
    unnamed x20, local copies, waits for them, and re-layouts  6.02 us

profile of v1, /device:TPU:1, one launch (start us, length us, event | category | flops | bytes accessed | tf_op | source)
XLA Modules:
  0.0 70.8 jit_solution(3253260411134117637)
XLA Ops:
  0.0 0.0 copy-start.6
  1.4 0.7 reshape.9.again_ref
  2.1 0.7 reshape.10.mgain_ref
  2.8 0.8 %copy.16.pt_ref.pt_s = s32[32,2]{1,0:T(8,128)S(1)} copy(s32[32,2]{0,1:T(2,128)} %param.24) | data formatting | bytes 512 | tf_op args[9]
  3.6 0.8 %copy.17.routes_ref = s32[48,6]{1,0:T(8,128)S(1)} copy(s32[48,6]{0,1:T(8,128)} %param.29) | data formatting | bytes 2304 | tf_op args[14]
  4.4 1.0 %copy.20.router_h = bf16[1536,8]{1,0:T(8,128)(2,1)S(1)} copy(bf16[1536,8]{0,1:T(8,128)(2,1)} %param.20) | data formatting | bytes 49152 | tf_op args[5]
  5.3 1.3 %copy.19.wqkv_h = bf16[1536,160]{1,0:T(8,128)(2,1)S(1)} copy(bf16[1536,160]{0,1:T(8,128)(2,1)} %param.17) | data formatting | bytes 983040 | tf_op args[2]
  6.6 0.0 copy-done.6
  6.6 0.0 copy-start
  6.6 0.0 copy-start.1
  6.7 0.0 copy-start.2
  6.7 0.0 copy-start.3
  6.7 0.0 copy-start.4
  6.7 0.0 copy-start.5
  6.7 0.4 copy.21
  7.1 1.0 %copy-done = bf16[6,2,128,512]{3,2,1,0:T(8,128)(2,1)S(1)} copy-done((bf16[6,2,128,512]{3,2,1,0:T(8,128)(2,1)S(1)}, bf16[6,2,128,512]{3,2,1,0:T(8,128)(2,1)}, u32[]{:S(2)}) %copy-start) | copy-done | bytes 1572888
  8.0 0.2 copy-done.1
  8.2 0.1 copy-done.2
  8.3 0.0 copy-done.3
  8.3 0.0 copy-done.4
  8.3 0.0 copy-done.5
  8.3 61.9 %shard_map.145 = bf16[3,1536]{1,0:T(4,128)(2,1)S(1)} custom-call(bf16[3,1536]{1,0:T(4,128)(2,1)S(1)} %copy-done.3, f32[1,1536]{1,0:T(1,128)S(1)} %reshape.9.again_ref, f32[1,1536]{1,0:T(1,128)S(1)} %reshape.10.mgain_ref, s32[32,2]{1,0:T(8,128)S(1)} %copy.16.pt_ref.pt_s, s32[48,6]{1,0:T(8,128)S(1)} %copy.17.routes_ref, s32[32,2]{1,0:T(8,128)S(1)} %copy.16.pt_ref.pt_s, ...), custom_call_target="tpu_custom_call" | custom-call | tf_op jit(solution)/shard_map/pallas_call | solution.py:459
  70.2 0.6 copy.25
Async XLA Ops:
  0.0 6.6 %copy-start.6 = (bf16[1536,2,256]{2,1,0:T(2,128)(2,1)S(1)}, bf16[1536,2,256]{2,1,0:T(2,128)(2,1)}, u32[]{:S(2)}) copy-start(bf16[1536,2,256]{2,1,0:T(2,128)(2,1)} %param.21) | copy-start | bytes 4718596
  6.6 1.4 %copy-start = (bf16[6,2,128,512]{3,2,1,0:T(8,128)(2,1)S(1)}, bf16[6,2,128,512]{3,2,1,0:T(8,128)(2,1)}, u32[]{:S(2)}) copy-start(bf16[6,2,128,512]{3,2,1,0:T(8,128)(2,1)} %kv_h.1) | copy-start | bytes 4718596
  6.6 1.6 %copy-start.1 = (bf16[256,1536]{1,0:T(8,128)(2,1)S(1)}, bf16[256,1536]{1,0:T(8,128)(2,1)}, u32[]{:S(2)}) copy-start(bf16[256,1536]{1,0:T(8,128)(2,1)} %wd_h.1) | copy-start | bytes 2359300
  6.7 1.6 %copy-start.2 = (bf16[96,1536]{1,0:T(8,128)(2,1)S(1)}, bf16[96,1536]{1,0:T(8,128)(2,1)}, u32[]{:S(2)}) copy-start(bf16[96,1536]{1,0:T(8,128)(2,1)} %wo_h.1) | copy-start | bytes 884740
  6.7 1.6 %copy-start.3 = (bf16[3,1536]{1,0:T(4,128)(2,1)S(1)}, bf16[3,1536]{1,0:T(4,128)(2,1)}, u32[]{:S(2)}) copy-start(bf16[3,1536]{1,0:T(4,128)(2,1)} %tok_ref.1) | copy-start | bytes 27652
  6.7 1.6 %copy-start.4 = (s32[32]{0:T(128)S(1)}, s32[32]{0:T(128)}, u32[]{:S(2)}) copy-start(s32[32]{0:T(128)} %hl_s.1) | copy-start | bytes 388
  6.7 1.6 %copy-start.5 = (s32[1,2]{1,0:T(1,128)S(1)}, s32[1,2]{1,0:T(1,128)}, u32[]{:S(2)}) copy-start(s32[1,2]{1,0:T(1,128)} %gp_s.1) | copy-start | bytes 28
